TPU v7x, 32 devices: a whole 2x2x4 slice. The times are simulated.
32 devices in a mesh: prow: 4 (over y, x), pcol: 8 (over z, core).
Axes of the slice: x: 2, y: 2, z: 4, core: 2. Of those that a mesh axis runs over, the one named last changes fastest.
Arguments:
- known_inverse: bfloat16 [4096, 4, 8, 128], P('prow', None, 'pcol'), may hold values from -6 to 6
- pattern: int32 [32, 4, 8, 1], P('prow', None, 'pcol'), may hold values 0 or 1
- panel_one: bfloat16 [4096, 512], P(('prow', 'pcol')), may hold values from -0.09375 to 0.09375
- panel_two: bfloat16 [4096, 512], P(('prow', 'pcol')), may hold values from -0.09375 to 0.09375
- panel_top: bfloat16 [512, 512], replicated, may hold values from -0.25 to 0.25
- structure: int32 [4096], P(('prow', 'pcol')), may hold values from 0 to 1, as said below
- diag_one: bfloat16 [512, 512], replicated, may hold values from -6 to 6
- diag_two: bfloat16 [512, 512], replicated, may hold values from -6 to 6
Outputs:
- inverse_one: bfloat16 [4096, 512], P(('prow', 'pcol'))
- corner_one: bfloat16 [512, 512], replicated
- inverse_top: bfloat16 [512, 512], replicated
- inverse_two: bfloat16 [4096, 512], P(('prow', 'pcol'))
- corner_two: bfloat16 [512, 512], replicated
Inputs may be any that keep to these rules, and one draw needn't show every extreme that they name: `structure`: in every aligned pair of rows (2 k and 2 k + 1) at least one entry is 1.
All inputs are finite; a program needn't handle non-finite values. No bound on the sum of `pattern` on one device may be relied on, other than what follows from the above.
Results may differ from a plain program's by a relative error of at most 0.0058.
Values may be sent and summed in bfloat16 or wider, within the bound.
No kernel may reach another device: no remote copies, remote signals or barrier semaphores. Data moves between devices by JAX's collectives and lax.ppermute only.
A program may use at most 128 MiB of HBM per device.

v0:
```python
import jax
import jax.numpy as jnp
from jax import lax
from jax.sharding import PartitionSpec as P

BLK = 128


def on_device(
    known_inverse, pattern, panel_one, panel_two, panel_top, structure, diag_one, diag_two
):
    row_count = known_inverse.shape[0]
    col_groups = known_inverse.shape[1]
    piece_rows = known_inverse.shape[3]
    width = panel_one.shape[1]
    block_rows = row_count // BLK
    piece_blocks = piece_rows // BLK
    shaped = known_inverse.reshape(block_rows, BLK, col_groups, piece_blocks, BLK)
    flag_table = pattern.reshape(block_rows, 1, col_groups, piece_blocks, 1)
    masked = jnp.where(flag_table > 0, shaped, jnp.zeros_like(shaped)).reshape(
        row_count, col_groups * piece_rows
    )
    row_flags = structure.reshape(piece_rows, 1) > 0
    masked_two = jnp.where(row_flags, panel_two, jnp.zeros_like(panel_two))
    partial_both = jnp.dot(
        masked,
        jnp.concatenate(
            (
                lax.all_gather(panel_one, "prow", axis=0, tiled=True),
                lax.all_gather(masked_two, "prow", axis=0, tiled=True),
            ),
            axis=1,
        ),
        preferred_element_type=jnp.float32,
    )
    reduced = lax.psum_scatter(partial_both, "pcol", scatter_dimension=0, tiled=True)
    reduced_one = reduced[:, :width]
    reduced_two = reduced[:, width:]
    inverse_one = (-reduced_one).astype(jnp.bfloat16)
    own_term = jnp.dot(panel_one.T, inverse_one, preferred_element_type=jnp.float32)
    cross_local = jnp.dot(inverse_one.T, masked_two, preferred_element_type=jnp.float32)
    lower_two = -(reduced_two + jnp.dot(inverse_one, panel_top, preferred_element_type=jnp.float32))
    inverse_two = jnp.where(row_flags, lower_two, jnp.zeros_like(lower_two)).astype(jnp.bfloat16)
    tail_local = jnp.dot(masked_two.T, inverse_two, preferred_element_type=jnp.float32)
    top_weights = panel_top.astype(jnp.float32)
    own_sum, cross_sum = lax.psum((own_term, cross_local), ("prow", "pcol"))
    corner_full = diag_one.astype(jnp.float32) - own_sum
    top_value = jnp.dot(corner_full, top_weights, precision=lax.Precision.HIGHEST) + cross_sum
    inverse_top = (-top_value).astype(jnp.bfloat16)
    tail_sum = lax.psum(tail_local, ("prow", "pcol"))
    corner_two = (
        diag_two.astype(jnp.float32)
        - jnp.dot(panel_top.T, inverse_top, preferred_element_type=jnp.float32)
        - tail_sum
    )
    return (
        inverse_one,
        corner_full.astype(jnp.bfloat16),
        inverse_top,
        inverse_two,
        corner_two.astype(jnp.bfloat16),
    )


def solution(mesh):
    in_specs = (
        P("prow", None, "pcol", None),
        P("prow", None, "pcol", None),
        P(("prow", "pcol"), None),
        P(("prow", "pcol"), None),
        P(),
        P(("prow", "pcol")),
        P(),
        P(),
    )
    out_specs = (P(("prow", "pcol"), None), P(), P(), P(("prow", "pcol"), None), P())
    return jax.shard_map(
        on_device, mesh=mesh, in_specs=in_specs, out_specs=out_specs, check_vma=False
    )
```

profile of v0, /device:TPU:0, one launch (start us, length us, event | category | flops | bytes accessed | tf_op | source)
XLA Modules:
  0.0 241.5 jit_solution(9505006935396776031)
XLA Ops:
  7.2 0.8 broadcast_compare_fusion.1
  8.0 1.0 broadcast_select_fusion
  9.0 11.5 %all_gather.7 = bf16[512,512]{1,0:T(8,128)(2,1)S(1)} all-gather(bf16[128,512]{1,0:T(8,128)(2,1)S(1)} %broadcast_select_fusion), channel_id=1, replica_groups=mesh['prow'=4,'pcol'=8] {'prow'}, dimensions={0}, use_global_device_ids=true | all-gather | bytes 655360 | tf_op jit(solution)/shard_map/all_gather | solution.py:30
  20.5 0.7 broadcast_compare_fusion
  21.2 0.1 copy.20
  21.3 10.7 %all_gather.6 = bf16[512,512]{1,0:T(8,128)(2,1)S(1)} all-gather(bf16[128,512]{1,0:T(8,128)(2,1)} %param.10), channel_id=1, replica_groups=mesh['prow'=4,'pcol'=8] {'prow'}, dimensions={0}, use_global_device_ids=true | all-gather | bytes 655360 | tf_op jit(solution)/shard_map/all_gather | solution.py:29
  32.0 0.3 broadcast_in_dim.33
  32.4 3.2 %fusion.8 = f32[1024,1024]{1,0:T(8,128)} fusion(pred[128,8,4,128]{3,2,1,0:T(4,128)(4,1)S(1)} %bitcast.36, bf16[128,8,4,128]{3,2,1,0:T(4,128)(2,1)S(1)} %bitcast.38, bf16[512,512]{1,0:T(8,128)(2,1)S(1)} %all_gather.7, bf16[512,512]{1,0:T(8,128)(2,1)S(1)} %all_gather.6), kind=kOutput, calls=%fused_computation.13 | convolution fusion | flops 1076363264 | bytes 6815744 | tf_op jit(solution)/shard_map/dot_general | solution.py:25
  35.7 50.3 %reduce-scatter.2.cloned.1.call-done = f32[128,1024]{1,0:T(8,128)} async-done(((f32[1024,1024]{1,0:T(8,128)}), f32[128,1024]{1,0:T(8,128)}) %reduce-scatter.2.cloned.1.call-update) | async-done | bytes 524304 | tf_op jit(solution)/shard_map/reduce_scatter | solution.py:36
  86.0 1.0 fusion.16
  87.0 1.3 fusion.19
  88.3 1.3 convolution_bitcast_fusion.1
  89.6 0.2 fusion.7
  89.9 1.4 fusion.20
  91.3 0.2 copy.14
  91.5 0.8 copy-done.8
  92.3 0.2 copy.15
  92.5 136.7 %all-reduce.3.cloned.1.call-done = (f32[512,512]{0,1:T(8,128)}, f32[512,512]{1,0:T(8,128)}, f32[512,512]{0,1:T(8,128)}) async-done(((f32[512,512]{0,1:T(8,128)}, f32[512,512]{1,0:T(8,128)}, f32[512,512]{0,1:T(8,128)}), (f32[512,512]{0,1:T(8,128)}, f32[512,512]{1,0:T(8,128)}, f32[512,512]{0,1:T(8,128)})) %all-reduce.3.cloned.1.call-update) | async-done | bytes 3145744 | tf_op jit(solution)/shard_map/psum | solution.py:46
  229.3 1.5 fusion.14
  230.8 0.3 copy-done.5
  231.1 1.0 fusion.3
  232.2 0.5 fusion.4
  232.6 1.0 copy.18
  233.7 1.0 copy.17
  (26 shorter events, 0.2 us)
Async XLA Ops:
  7.2 82.5 %copy-start = (bf16[512,512]{1,0:T(8,128)(2,1)S(1)}, bf16[512,512]{1,0:T(8,128)(2,1)}, u32[]{:S(2)}) copy-start(bf16[512,512]{1,0:T(8,128)(2,1)} %param.12) | copy-start | bytes 1572868
  7.2 25.2 %copy-start.11 = (bf16[1024,4,1,128]{3,1,2,0:T(4,128)(2,1)S(1)}, bf16[1024,4,1,128]{3,1,2,0:T(4,128)(2,1)}, u32[]{:S(2)}) copy-start(bf16[1024,4,1,128]{3,1,2,0:T(4,128)(2,1)} %param.8) | copy-start | bytes 3145732
  7.2 78.8 %reduce-scatter.2.cloned.1.call-start = ((), (), s32[]{:S(2)}) async-start(), calls=%async_computation.1 | async-start | bytes 4718592 | tf_op jit(solution)/shard_map/reduce_scatter | solution.py:36
  35.6 52.7 %copy-start.6 = (bf16[128,512]{1,0:T(8,128)(2,1)S(1)}, bf16[128,512]{1,0:T(8,128)(2,1)}, u32[]{:S(2)}) copy-start(bf16[128,512]{1,0:T(8,128)(2,1)} %param.10) | copy-start | bytes 393220
  35.6 193.6 %all-reduce.3.cloned.1.call-start = ((), (), s32[]{:S(2)}) async-start(), calls=%async_computation.2 | async-start | bytes 6291456 | tf_op jit(solution)/shard_map/psum | solution.py:46
  86.0 3.7 %copy-start.9 = (f32[128,1024]{1,0:T(8,128)S(1)}, f32[128,1024]{1,0:T(8,128)}, u32[]{:S(2)}) copy-start(f32[128,1024]{1,0:T(8,128)} %reduce-scatter.2.cloned.1.call-done) | copy-start | bytes 1572868
  87.0 4.3 %copy-start.3 = (bf16[128,512]{1,0:T(8,128)(2,1)}, bf16[128,512]{1,0:T(8,128)(2,1)S(1)}, u32[]{:S(2)}) copy-start(bf16[128,512]{1,0:T(8,128)(2,1)S(1)} %fusion.16) | copy-start | bytes 393220
  89.9 1.4 copy-start.10
  89.9 1.4 copy-start.7
  91.3 1.0 copy-start.8
  229.3 1.6 copy-start.1
  229.3 1.9 copy-start.5
  230.8 1.4 copy-start.4
  232.1 1.5 copy-start.2
Sparse Core Ops, SparseCore 0:
  35.8 50.1 reduce-scatter.1
  91.8 137.4 all-reduce.2
where the time goes:
time: 242 us; the launch traced here: 241 us
  waiting for transfers between devices  187 us (77%)
  blocking collectives  22.2 us (9%)
  between operations  14.2 us (6%)
  matrix products  8.95 us (4%)
  other arithmetic  5.02 us (2%)
  local copies, waits for them, and re-layouts  4.01 us (2%)
    psum x1, waiting for transfers between devices, on_device(): own_sum, cross_sum = lax.psum((own_term, cross_local), ('prow', 'pcol'))  137 us
    reduce_scatter x1, waiting for transfers between devices, on_device(): lax.psum_scatter(partial_both, 'pcol', scatter_dimension=0, tiled=True)  50.3 us
    all_gather x1, blocking collectives, on_device(): lax.all_gather(masked_two, 'prow', axis=0, tiled=True)  11.5 us
    all_gather x1, blocking collectives, on_device(): lax.all_gather(panel_one, 'prow', axis=0, tiled=True)  10.7 us
  transfers between devices with their start and end apart: 2, of which 2 were waited for; matrix products, arithmetic and copies ran while one was open for 0% of the time, Pallas kernels for 0%

commit v1 on v0

--- a/solution.py
+++ b/solution.py
@@ -43,7 +43,7 @@
     inverse_two = jnp.where(row_flags, lower_two, jnp.zeros_like(lower_two)).astype(jnp.bfloat16)
     tail_local = jnp.dot(masked_two.T, inverse_two, preferred_element_type=jnp.float32)
     top_weights = panel_top.astype(jnp.float32)
-    own_sum, cross_sum = lax.psum((own_term, cross_local), ("prow", "pcol"))
+    own_sum, cross_sum = lax.psum(lax.psum((own_term, cross_local), "pcol"), "prow")
     corner_full = diag_one.astype(jnp.float32) - own_sum
     top_value = jnp.dot(corner_full, top_weights, precision=lax.Precision.HIGHEST) + cross_sum
     inverse_top = (-top_value).astype(jnp.bfloat16)

time: 242 us -> 372 us (1.54)
  waiting for transfers between devices: 187 us -> 317 us
    psum x1 -> x3, waiting for transfers between devices: 137 us -> 266 us  [the longest x1 133 us: on_device(): tail_sum = lax.psum(tail_local, ('prow', 'pcol'))]
  transfers between devices with their start and end apart: 2 -> 4, of which waited for: 2 -> 4; matrix products, arithmetic and copies ran while one was open for 0% -> 1% of each run, Pallas kernels for 0% -> 0%
where the time goes in v1:
time: 372 us
  waiting for transfers between devices  317 us (85%)
  blocking collectives  22.2 us (6%)
  between operations  13.9 us (4%)
  matrix products  10.1 us (3%)
  other arithmetic  4.95 us (1%)
  local copies, waits for them, and re-layouts  3.72 us (1%)
    psum x1, waiting for transfers between devices, on_device(): tail_sum = lax.psum(tail_local, ('prow', 'pcol'))  133 us
    psum x1, waiting for transfers between devices, on_device(): lax.psum(lax.psum((own_term, cross_local), 'pcol'), 'prow')  69.6 us
    psum x1, waiting for transfers between devices, on_device(): lax.psum((own_term, cross_local), 'pcol')  63.8 us
    reduce_scatter x1, waiting for transfers between devices, on_device(): lax.psum_scatter(partial_both, 'pcol', scatter_dimension=0, tiled=True)  50.3 us
    all_gather x1, blocking collectives, on_device(): lax.all_gather(masked_two, 'prow', axis=0, tiled=True)  11.5 us
    all_gather x1, blocking collectives, on_device(): lax.all_gather(panel_one, 'prow', axis=0, tiled=True)  10.7 us
  transfers between devices with their start and end apart: 4, of which 4 were waited for; matrix products, arithmetic and copies ran while one was open for 1% of the time, Pallas kernels for 0%

profile of v1, /device:TPU:0, one launch (start us, length us, event | category | flops | bytes accessed | tf_op | source)
XLA Modules:
  0.0 371.7 jit_solution(2221398023934157617)
XLA Ops:
  7.2 0.8 broadcast_compare_fusion.1
  8.0 1.0 broadcast_select_fusion
  9.0 11.5 %all_gather.7 = bf16[512,512]{1,0:T(8,128)(2,1)S(1)} all-gather(bf16[128,512]{1,0:T(8,128)(2,1)S(1)} %broadcast_select_fusion), channel_id=1, replica_groups=mesh['prow'=4,'pcol'=8] {'prow'}, dimensions={0}, use_global_device_ids=true | all-gather | bytes 655360 | tf_op jit(solution)/shard_map/all_gather | solution.py:30
  20.5 0.7 broadcast_compare_fusion
  21.3 10.7 %all_gather.6 = bf16[512,512]{1,0:T(8,128)(2,1)S(1)} all-gather(bf16[128,512]{1,0:T(8,128)(2,1)} %param.10), channel_id=1, replica_groups=mesh['prow'=4,'pcol'=8] {'prow'}, dimensions={0}, use_global_device_ids=true | all-gather | bytes 655360 | tf_op jit(solution)/shard_map/all_gather | solution.py:29
  32.0 0.3 broadcast_in_dim.33
  32.4 3.2 fusion.8
  35.7 50.3 %reduce-scatter.2.cloned.1.call-done = f32[128,1024]{1,0:T(8,128)} async-done(((f32[1024,1024]{1,0:T(8,128)}), f32[128,1024]{1,0:T(8,128)}) %reduce-scatter.2.cloned.1.call-update) | async-done | bytes 524304 | tf_op jit(solution)/shard_map/reduce_scatter | solution.py:36
  86.0 1.0 fusion.16
  86.9 1.3 fusion.19
  88.3 1.3 convolution_bitcast_fusion.1
  89.6 63.8 %all-reduce.8.cloned.1.call-done = (f32[512,512]{0,1:T(8,128)}, f32[512,512]{1,0:T(8,128)}) async-done(((f32[512,512]{0,1:T(8,128)}, f32[512,512]{1,0:T(8,128)}), (f32[512,512]{0,1:T(8,128)}, f32[512,512]{1,0:T(8,128)})) %all-reduce.8.cloned.1.call-update) | async-done | bytes 2097168 | tf_op jit(solution)/shard_map/psum | solution.py:46
  153.5 0.2 copy.14
  154.0 0.5 copy-done.8
  154.5 0.2 fusion.7
  154.7 1.3 fusion.20
  156.1 69.6 %all-reduce.10.cloned.1.call-done = (f32[512,512]{0,1:T(8,128)}, f32[512,512]{1,0:T(8,128)}) async-done(((f32[512,512]{0,1:T(8,128)}, f32[512,512]{1,0:T(8,128)}), (f32[512,512]{0,1:T(8,128)}, f32[512,512]{1,0:T(8,128)})) %all-reduce.10.cloned.1.call-update) | async-done | bytes 2097168 | tf_op jit(solution)/shard_map/psum | solution.py:46
  225.7 1.5 fusion.14
  227.3 0.3 copy-done.4
  227.6 1.0 fusion.3
  228.6 132.8 %all-reduce.6.cloned.1.call-done = f32[512,512]{0,1:T(8,128)} async-done(((f32[512,512]{0,1:T(8,128)}), f32[512,512]{0,1:T(8,128)}) %all-reduce.6.cloned.1.call-update) | async-done | bytes 1048592 | tf_op jit(solution)/shard_map/psum | solution.py:50
  361.4 1.7 fusion.4
  363.1 1.0 copy.18
  364.1 1.0 copy.17
  (30 shorter events, 0.6 us)
Async XLA Ops:
  7.2 146.8 %copy-start = (bf16[512,512]{1,0:T(8,128)(2,1)S(1)}, bf16[512,512]{1,0:T(8,128)(2,1)}, u32[]{:S(2)}) copy-start(bf16[512,512]{1,0:T(8,128)(2,1)} %param.12) | copy-start | bytes 1572868
  7.2 25.2 %copy-start.10 = (bf16[1024,4,1,128]{3,1,2,0:T(4,128)(2,1)S(1)}, bf16[1024,4,1,128]{3,1,2,0:T(4,128)(2,1)}, u32[]{:S(2)}) copy-start(bf16[1024,4,1,128]{3,1,2,0:T(4,128)(2,1)} %param.8) | copy-start | bytes 3145732
  7.2 78.8 %reduce-scatter.2.cloned.1.call-start = ((), (), s32[]{:S(2)}) async-start(), calls=%async_computation.1 | async-start | bytes 4718592 | tf_op jit(solution)/shard_map/reduce_scatter | solution.py:36
  35.6 52.7 %copy-start.5 = (bf16[128,512]{1,0:T(8,128)(2,1)S(1)}, bf16[128,512]{1,0:T(8,128)(2,1)}, u32[]{:S(2)}) copy-start(bf16[128,512]{1,0:T(8,128)(2,1)} %param.10) | copy-start | bytes 393220
  35.6 117.8 %all-reduce.8.cloned.1.call-start = ((), (), s32[]{:S(2)}) async-start(), calls=%async_computation.3 | async-start | bytes 4194304 | tf_op jit(solution)/shard_map/psum | solution.py:46
  86.9 67.1 %copy-start.3 = (bf16[128,512]{1,0:T(8,128)(2,1)}, bf16[128,512]{1,0:T(8,128)(2,1)S(1)}, u32[]{:S(2)}) copy-start(bf16[128,512]{1,0:T(8,128)(2,1)S(1)} %fusion.16) | copy-start | bytes 393220
  89.6 64.0 %copy-start.6 = (bf16[512,512]{1,0:T(8,128)(2,1)S(1)}, bf16[512,512]{1,0:T(8,128)(2,1)}, u32[]{:S(2)}) copy-start(bf16[512,512]{1,0:T(8,128)(2,1)} %param.14) | copy-start | bytes 1572868
  89.6 64.2 %copy-start.7 = (bf16[512,512]{1,0:T(8,128)(2,1)S(1)}, bf16[512,512]{1,0:T(8,128)(2,1)}, u32[]{:S(2)}) copy-start(bf16[512,512]{1,0:T(8,128)(2,1)} %param.15) | copy-start | bytes 1572868
  89.6 136.1 %all-reduce.10.cloned.1.call-start = ((), (), s32[]{:S(2)}) async-start(), calls=%async_computation.4 | async-start | bytes 4194304 | tf_op jit(solution)/shard_map/psum | solution.py:46
  153.5 1.0 copy-start.8
  153.5 207.9 %all-reduce.6.cloned.1.call-start = ((), (), s32[]{:S(2)}) async-start(), calls=%async_computation.2 | async-start | bytes 2097152 | tf_op jit(solution)/shard_map/psum | solution.py:50
  154.7 72.5 %copy-start.9 = (bf16[128,512]{1,0:T(8,128)(2,1)}, bf16[128,512]{1,0:T(8,128)(2,1)S(1)}, u32[]{:S(2)}) copy-start(bf16[128,512]{1,0:T(8,128)(2,1)S(1)} %fusion.7) | copy-start | bytes 393220
  225.7 1.6 copy-start.1
  225.7 1.9 copy-start.4
  228.6 135.5 %copy-start.2 = (bf16[512,512]{1,0:T(8,128)(2,1)}, bf16[512,512]{1,0:T(8,128)(2,1)S(1)}, u32[]{:S(2)}) copy-start(bf16[512,512]{1,0:T(8,128)(2,1)S(1)} %fusion.3) | copy-start | bytes 1572868
Sparse Core Ops, SparseCore 0:
  35.7 50.1 reduce-scatter.1
  89.7 63.7 all-reduce.7
  156.5 69.1 all-reduce.9
  230.8 130.6 all-reduce.5
